TPU v7x, 128 devices: a whole 4x4x4 slice. The times are simulated.
128 devices in a mesh: dev: 128 (over z, y, x, core).
Axes of the slice: x: 4, y: 4, z: 4, core: 2. Of those that a mesh axis runs over, the one named last changes fastest.
Arguments:
- source: bfloat16 [16384, 1024], P('dev'), may hold values from -17 to 17
- target: bfloat16 [16384, 1024], P('dev'), may hold values from -17 to 17
- partner: int32 [2, 128], replicated, may hold values from 0 to 127, as said below
Outputs:
- src_aligned: bfloat16 [16384, 1024], P('dev')
- tgt_aligned: bfloat16 [16384, 1024], P('dev')
- src_lse: float32 [16384], P('dev')
- tgt_lse: float32 [16384], P('dev')
Inputs may be any that keep to these rules, and one draw needn't show every extreme that they name: Row r of partner is round r of one round-robin tournament among the 128 blocks: partner[r, partner[r, b]] = b and partner[r, b] != b; the rows are distinct rounds.
All inputs are finite; a program needn't handle non-finite values.
Results may differ from a plain program's by a relative error of at most 0.0018.
Values may be sent and summed in bfloat16 or wider, within the bound.
A program may use at most 64 MiB of HBM per device.

v0:
```python
import jax
import jax.numpy as jnp
from jax import lax
from jax.sharding import PartitionSpec as P


def sent_together(arrays, axis, split_dim, concat_dim, along):
    widths = [a.shape[along] for a in arrays]
    both = jnp.concatenate(arrays, axis=along)
    whole = lax.all_to_all(both, axis, split_axis=split_dim, concat_axis=concat_dim, tiled=True)
    return tuple(jnp.split(whole, [sum(widths[:k]) for k in range(1, len(widths))], axis=along))


def attend(queries, values, factor):
    scores = (
        lax.dot_general(
            queries, values, (((1,), (1,)), ((), ())), preferred_element_type=jnp.float32
        )
        * factor
    )
    highest = jnp.max(scores, axis=1)
    weights = jnp.exp(scores - highest[:, None])
    summed_weights = jnp.sum(weights, axis=1)
    weighted = jnp.dot(weights.astype(jnp.bfloat16), values, preferred_element_type=jnp.float32)
    return (highest, summed_weights, weighted)


def stack_results(results):
    return tuple((jnp.stack([entry[member] for entry in results]) for member in range(6)))


def merge_rounds(highest, summed_weights, weighted):
    peak = highest[0]
    turn = 1
    peak = jnp.maximum(peak, highest[turn])
    denominator = jnp.zeros_like(peak)
    numerator = jnp.zeros_like(weighted[0])
    for turn in range(highest.shape[0]):
        factor = jnp.exp(highest[turn] - peak)
        denominator = denominator + factor * summed_weights[turn]
        numerator = numerator + factor[:, None] * weighted[turn]
    return ((numerator / denominator[:, None]).astype(jnp.bfloat16), peak + jnp.log(denominator))


def local(source, target, partner):
    blocks = lax.axis_size("dev")
    row_count, width_count = source.shape
    slab_rows = row_count // blocks
    factor = width_count ** (-0.5)
    numbers = jnp.arange(blocks, dtype=jnp.int32)

    def invert_row(order):
        return jnp.zeros((blocks,), jnp.int32).at[order].set(numbers)

    inverse = jax.vmap(invert_row)(partner)
    held_targets, held_sources = sent_together(
        (
            target.reshape(blocks, slab_rows, width_count),
            source.reshape(blocks, slab_rows, width_count),
        ),
        "dev",
        0,
        0,
        1,
    )
    outgoing_targets = jnp.take(held_targets, partner, axis=0)
    outgoing_sources = jnp.take(held_sources, inverse, axis=0)
    arrived_targets = lax.all_to_all(
        outgoing_targets, "dev", split_axis=1, concat_axis=1, tiled=True
    )
    arrived_sources = lax.all_to_all(
        outgoing_sources, "dev", split_axis=1, concat_axis=1, tiled=True
    )
    results = []
    for position in range(arrived_targets.shape[0]):
        partner_targets = arrived_targets[position].reshape(row_count, width_count)
        partner_sources = arrived_sources[position].reshape(row_count, width_count)
        results.append(
            attend(source, partner_targets, factor) + attend(target, partner_sources, factor)
        )
    outcome = stack_results(results)
    forward = outcome[:3]
    backward = outcome[3:]
    src_aligned, src_lse = merge_rounds(forward[0], forward[1], forward[2])
    tgt_aligned, tgt_lse = merge_rounds(backward[0], backward[1], backward[2])
    return (src_aligned, tgt_aligned, src_lse, tgt_lse)


def solution(mesh):
    placed = (P("dev", None), P("dev", None), P())
    return jax.shard_map(
        local,
        mesh=mesh,
        in_specs=placed,
        out_specs=(P("dev", None), P("dev", None), P("dev"), P("dev")),
        check_vma=False,
    )
```

profile of v0, /device:TPU:1, one launch (start us, length us, event | category | flops | bytes accessed | tf_op | source)
XLA Modules:
  0.0 76.5 jit_solution(1740895637635163958)
XLA Ops:
  0.6 1.1 %pad_maximum_fusion = bf16[128,2,1024]{2,0,1:T(8,128)(2,1)S(1)} fusion(bf16[128,1,1024]{2,0,1:T(8,128)(2,1)} %bitcast.47, bf16[128,1,1024]{2,0,1:T(8,128)(2,1)} %bitcast.46), kind=kLoop, calls=%fused_computation.19 | loop fusion | flops 262144 | bytes 1048576 | tf_op jit(solution)/shard_map/concatenate | solution.py:9
  1.7 1.3 %copy.14 = bf16[128,2,1024]{2,1,0:T(2,128)(2,1)} copy(bf16[128,2,1024]{2,0,1:T(8,128)(2,1)S(1)} %pad_maximum_fusion) | data formatting | bytes 1048576 | tf_op jit(solution)/shard_map/concatenate | solution.py:9
  3.0 11.5 %all-to-all-start = ((bf16[128,2,1024]{2,1,0:T(2,128)(2,1)}), bf16[128,2,1024]{2,1,0:T(2,128)(2,1)S(1)}, u32[]{:S(2)}, u32[]{:S(2)}) async-start(bf16[128,2,1024]{2,1,0:T(2,128)(2,1)} %copy.14), calls=%async_computation | async-start | bytes 1048576 | tf_op jit(solution)/shard_map/all_to_all | solution.py:10
  14.6 0.7 copy-done.2
  15.2 11.4 %scatter_fusion = s32[2,128]{1,0:T(2,128)S(1)} fusion(s32[2,128]{1,0:T(2,128)S(1)} %lt.12, s32[256]{0:T(256)S(1)} %fusion.24, s32[256]{0:T(256)S(1)} %iota_bitcast_fusion), kind=kCustom, calls=%fused_computation.2 | custom fusion | bytes 5120 | tf_op jit(solution)/shard_map/vmap()/scatter | solution.py:53
  27.0 1.3 %all-to-all-done = bf16[128,2,1024]{2,1,0:T(2,128)(2,1)S(1)} async-done(((bf16[128,2,1024]{2,1,0:T(2,128)(2,1)}), bf16[128,2,1024]{2,1,0:T(2,128)(2,1)S(1)}, u32[]{:S(2)}, u32[]{:S(2)}) %all-to-all-start) | async-done | bytes 524320 | tf_op jit(solution)/shard_map/all_to_all | solution.py:10
  28.3 0.7 fusion.28
  29.2 1.2 %gather_fusion.1 = bf16[256,1024]{1,0:T(8,128)(2,1)S(1)} fusion(bf16[128,1024]{1,0:T(8,128)(2,1)S(1)} %get-tuple-element.27, s32[1024]{0:T(1024)S(1)} %pad_clamp_fusion), kind=kCustom, calls=%fused_computation.1.clone | custom fusion | bytes 1049600 | tf_op jit(solution)/shard_map/jit(_take)/gather | solution.py:67
  30.4 1.5 %broadcast_select_fusion = bf16[2,128,1,1024]{3,0,2,1:T(2,128)(2,1)} fusion(pred[2,128]{0,1:T(8,128)(4,1)S(1)} %copy.19, bf16[2,128,1,1024]{3,1,0,2:T(8,128)(2,1)S(1)} %bitcast.48), kind=kLoop, calls=%fused_computation.17 | loop fusion | flops 262144 | bytes 1048832 | tf_op jit(solution)/shard_map/jit(_take)/select_n | solution.py:67
  31.9 8.5 %all-to-all-start.2 = ((bf16[2,128,1,1024]{3,0,2,1:T(2,128)(2,1)}), bf16[2,128,1,1024]{3,0,2,1:T(2,128)(2,1)S(1)}, u32[]{:S(2)}, u32[]{:S(2)}) async-start(bf16[2,128,1,1024]{3,0,2,1:T(2,128)(2,1)} %broadcast_select_fusion), calls=%async_computation.2 | async-start | bytes 1048576 | tf_op jit(solution)/shard_map/all_to_all | solution.py:71
  40.4 1.2 %gather_fusion = bf16[256,1024]{1,0:T(8,128)(2,1)S(1)} fusion(bf16[128,1024]{1,0:T(8,128)(2,1)S(1)} %get-tuple-element.28, s32[1024]{0:T(1024)S(1)} %pad_clamp_fusion.1), kind=kCustom, calls=%fused_computation.clone | custom fusion | bytes 1049600 | tf_op jit(solution)/shard_map/jit(_take)/gather | solution.py:66
  41.6 1.5 %broadcast_select_fusion.1 = bf16[2,128,1,1024]{3,0,2,1:T(2,128)(2,1)} fusion(pred[2,128]{0,1:T(8,128)(4,1)S(1)} %copy.13, bf16[2,128,1,1024]{3,1,0,2:T(8,128)(2,1)S(1)} %bitcast.49), kind=kLoop, calls=%fused_computation.18 | loop fusion | flops 262144 | bytes 1048832 | tf_op jit(solution)/shard_map/jit(_take)/select_n | solution.py:66
  43.1 11.0 %all-to-all-done.2 = bf16[2,128,1,1024]{3,0,2,1:T(2,128)(2,1)S(1)} async-done(((bf16[2,128,1,1024]{3,0,2,1:T(2,128)(2,1)}), bf16[2,128,1,1024]{3,0,2,1:T(2,128)(2,1)S(1)}, u32[]{:S(2)}, u32[]{:S(2)}) %all-to-all-start.2) | async-done | bytes 524320 | tf_op jit(solution)/shard_map/all_to_all | solution.py:71
  54.1 4.5 %all-to-all-start.1 = ((bf16[2,128,1,1024]{3,0,2,1:T(2,128)(2,1)}), bf16[2,128,1,1024]{3,0,2,1:T(2,128)(2,1)S(1)}, u32[]{:S(2)}, u32[]{:S(2)}) async-start(bf16[2,128,1,1024]{3,0,2,1:T(2,128)(2,1)} %broadcast_select_fusion.1), calls=%async_computation.1 | async-start | bytes 1048576 | tf_op jit(solution)/shard_map/all_to_all | solution.py:68
  58.7 0.7 fusion.27
  59.8 0.3 fusion.33
  60.2 0.5 log_add_fusion
  60.7 0.3 convolution_multiply_fusion
  61.0 11.4 %all-to-all-done.1 = bf16[2,128,1,1024]{3,0,2,1:T(2,128)(2,1)S(1)} async-done(((bf16[2,128,1,1024]{3,0,2,1:T(2,128)(2,1)}), bf16[2,128,1,1024]{3,0,2,1:T(2,128)(2,1)S(1)}, u32[]{:S(2)}, u32[]{:S(2)}) %all-to-all-start.1) | async-done | bytes 524320 | tf_op jit(solution)/shard_map/all_to_all | solution.py:68
  72.4 0.7 fusion.29
  73.7 0.5 log_add_fusion.1
  74.2 0.3 convolution_multiply_fusion.2
  74.5 1.0 %fusion.4 = bf16[128,1024]{1,0:T(8,128)(2,1)} fusion(f32[128,1024]{1,0:T(8,128)S(1)} %convolution_multiply_fusion, f32[128]{0:T(128)S(1)} %get-tuple-element.6, f32[128]{0:T(128)S(1)} %get-tuple-element.7, bf16[1,128,1,1024]{3,0,2,1:T(2,128)(2,1)S(1)} %get-tuple-element.14, f32[128,128]{1,0:T(8,128)S(1)} %get-tuple-element.24, f32[128]{0:T(128)S(1)} %get-tuple-element.23), kind=kOutput, calls=%fused_computation.11 | convolution fusion | flops 34111488 | bytes 1115648 | tf_op jit(solution)/shard_map/dot_general | solution.py:24
  75.5 1.0 %fusion.5 = bf16[128,1024]{1,0:T(8,128)(2,1)} fusion(f32[128,1024]{1,0:T(8,128)S(1)} %convolution_multiply_fusion.2, f32[128]{0:T(128)S(1)} %get-tuple-element.10, f32[128]{0:T(128)S(1)} %get-tuple-element.11, bf16[1,128,1,1024]{3,0,2,1:T(2,128)(2,1)S(1)} %get-tuple-element.18, f32[128,128]{1,0:T(8,128)S(1)} %get-tuple-element.20, f32[128]{0:T(128)S(1)} %get-tuple-element.19), kind=kOutput, calls=%fused_computation.12 | convolution fusion | flops 34111488 | bytes 1115648 | tf_op jit(solution)/shard_map/dot_general | solution.py:24
  (24 shorter events, 1.6 us)
Async XLA Ops:
  3.0 25.2 %all-to-all-start = ((bf16[128,2,1024]{2,1,0:T(2,128)(2,1)}), bf16[128,2,1024]{2,1,0:T(2,128)(2,1)S(1)}, u32[]{:S(2)}, u32[]{:S(2)}) async-start(bf16[128,2,1024]{2,1,0:T(2,128)(2,1)} %copy.14), calls=%async_computation | async-start | bytes 1048576 | tf_op jit(solution)/shard_map/all_to_all | solution.py:10
  14.5 0.7 copy-start.2
  31.9 22.3 %all-to-all-start.2 = ((bf16[2,128,1,1024]{3,0,2,1:T(2,128)(2,1)}), bf16[2,128,1,1024]{3,0,2,1:T(2,128)(2,1)S(1)}, u32[]{:S(2)}, u32[]{:S(2)}) async-start(bf16[2,128,1,1024]{3,0,2,1:T(2,128)(2,1)} %broadcast_select_fusion), calls=%async_computation.2 | async-start | bytes 1048576 | tf_op jit(solution)/shard_map/all_to_all | solution.py:71
  54.1 18.2 %all-to-all-start.1 = ((bf16[2,128,1,1024]{3,0,2,1:T(2,128)(2,1)}), bf16[2,128,1,1024]{3,0,2,1:T(2,128)(2,1)S(1)}, u32[]{:S(2)}, u32[]{:S(2)}) async-start(bf16[2,128,1,1024]{3,0,2,1:T(2,128)(2,1)} %broadcast_select_fusion.1), calls=%async_computation.1 | async-start | bytes 1048576 | tf_op jit(solution)/shard_map/all_to_all | solution.py:68
  58.6 1.0 %copy-start = (bf16[128,1024]{1,0:T(8,128)(2,1)S(1)}, bf16[128,1024]{1,0:T(8,128)(2,1)}, u32[]{:S(2)}) copy-start(bf16[128,1024]{1,0:T(8,128)(2,1)} %param.6) | copy-start | bytes 786436
  61.0 12.1 %copy-start.1 = (bf16[128,1024]{1,0:T(8,128)(2,1)S(1)}, bf16[128,1024]{1,0:T(8,128)(2,1)}, u32[]{:S(2)}) copy-start(bf16[128,1024]{1,0:T(8,128)(2,1)} %param.5) | copy-start | bytes 786436
where the time goes:
time: 76.8 us; the launch traced here: 76.5 us
  starting transfers between devices  24.5 us (32%)
  waiting for transfers between devices  23.7 us (31%)
  local copies, waits for them, and re-layouts  18.6 us (24%)
  other arithmetic  5.37 us (7%)
  matrix products  3.47 us (5%)
  between operations  0.8 us (1%)
    all_to_all x1, starting transfers between devices, sent_together(): lax.all_to_all(both, axis, split_axis=split_dim, concat_axis=concat_dim,...  11.5 us
    scatter x1, local copies, waits for them, and re-layouts, invert_row(): return jnp.zeros((blocks,), jnp.int32).at[order].set(numbers)  11.4 us
    all_to_all x1, waiting for transfers between devices, local(): lax.all_to_all(outgoing_targets, 'dev', split_axis=1, concat_axis=1, tile...  11.4 us
    all_to_all x1, waiting for transfers between devices, local(): lax.all_to_all(outgoing_sources, 'dev', split_axis=1, concat_axis=1, tile...  11 us
    all_to_all x1, starting transfers between devices, local(): lax.all_to_all(outgoing_sources, 'dev', split_axis=1, concat_axis=1, tile...  8.52 us
    all_to_all x1, starting transfers between devices, local(): lax.all_to_all(outgoing_targets, 'dev', split_axis=1, concat_axis=1, tile...  4.51 us
    dot_general x4, matrix products, attend(): jnp.dot(weights.astype(jnp.bfloat16), values, preferred_element_type=jnp....  2.47 us
  transfers between devices with their start and end apart: 3, of which 3 were waited for; matrix products, arithmetic and copies ran while one was open for 22% of the time, Pallas kernels for 0%

commit v1 on v0

v1 whole, which is shorter than its diff:
```python
import functools

import jax
import jax.numpy as jnp
from jax import lax
from jax.experimental import pallas as pl
from jax.experimental.pallas import tpu as pltpu
from jax.sharding import PartitionSpec as P

MESH = pl.DeviceIdType.MESH
BF, F32 = jnp.bfloat16, jnp.float32


def tile(chip):
    row = pl.multiple_of(lax.div(chip, 8) * 16, 16)
    column = pl.multiple_of(lax.rem(chip, 8) * 128, 128)
    return pl.ds(row, 16), pl.ds(column, 128)


def attend(queries, values, factor):
    scores = lax.dot_general(
        queries, values, (((1,), (1,)), ((), ())), preferred_element_type=F32
    ) * factor
    highest = jnp.max(scores, axis=1, keepdims=True)
    weights = jnp.exp(scores - highest)
    total = jnp.sum(weights, axis=1, keepdims=True)
    summed = jnp.dot(weights.astype(BF), values, preferred_element_type=F32)
    return highest, total, summed


def to_row(column):
    rows = column.shape[0]
    at_row = lax.broadcasted_iota(jnp.int32, (rows, rows), 0)
    at_column = lax.broadcasted_iota(jnp.int32, (rows, rows), 1)
    spread = jnp.where(at_row == at_column, jnp.broadcast_to(column, (rows, rows)), 0.0)
    return jnp.sum(spread, axis=0, keepdims=True)


def side(query_ref, got, which, aligned_ref, lse_ref, factor):
    queries = query_ref[...]
    m0, t0, w0 = attend(queries, got[which, 0], factor)
    m1, t1, w1 = attend(queries, got[which, 1], factor)
    peak = jnp.maximum(m0, m1)
    f0, f1 = jnp.exp(m0 - peak), jnp.exp(m1 - peak)
    den = f0 * t0 + f1 * t1
    aligned_ref[...] = ((f0 * w0 + f1 * w1) / den).astype(BF)
    lse_ref[...] = to_row(peak + jnp.log(den))


def kernel(
    devices, factor, partner, s_ref, t_ref, so_ref, to_ref, sl_ref, tl_ref,
    held, stage, got, send1, recv1, send2, recv2, own_sem,
):
    chips = devices // 2
    me = lax.axis_index("dev")
    chip, core = lax.div(me, 2), lax.rem(me, 2)

    barrier = pltpu.get_barrier_semaphore()

    @pl.loop(1, devices)
    def _(k):
        pl.semaphore_signal(
            barrier, inc=1, device_id=(lax.rem(me + k, devices),), device_id_type=MESH
        )

    pl.semaphore_wait(barrier, devices - 1)

    def spread(ref, to_chip, to_core):
        rows, columns = tile(to_chip)
        return pltpu.make_async_remote_copy(
            src_ref=ref.at[rows, columns],
            dst_ref=held.at[me],
            send_sem=send1,
            recv_sem=recv1,
            device_id=(2 * to_chip + to_core,),
            device_id_type=MESH,
        )

    rows, columns = tile(chip)

    @pl.when(core == 0)
    def _():
        spread(t_ref, chip, 1).start()
        held[me] = s_ref[rows, columns]

    @pl.when(core == 1)
    def _():
        spread(s_ref, chip, 0).start()
        held[me] = t_ref[rows, columns]

    @pl.loop(1, chips)
    def _(k):
        to_chip = lax.rem(chip + k, chips)
        spread(s_ref, to_chip, 0).start()
        spread(t_ref, to_chip, 1).start()

    whole1 = held.at[pl.ds(0, devices - 1)]
    wait1 = pltpu.make_async_remote_copy(
        src_ref=whole1, dst_ref=whole1, send_sem=send1, recv_sem=recv1,
        device_id=(lax.rem(me + 1, devices),), device_id_type=MESH,
    )
    wait1.wait_recv()

    @pl.loop(1, devices)
    def _(k):
        j = lax.rem(me + k, devices)
        stage[j, 0] = held[partner[0, j]]
        stage[j, 1] = held[partner[1, j]]
        pltpu.make_async_remote_copy(
            src_ref=stage.at[j],
            dst_ref=got.at[core, :, rows, columns],
            send_sem=send2,
            recv_sem=recv2,
            device_id=(j,),
            device_id_type=MESH,
        ).start()

    got[core, 0, rows, columns] = held[partner[0, me]]
    got[core, 1, rows, columns] = held[partner[1, me]]
    whole2 = stage.at[pl.ds(0, devices - 1)]
    wait2 = pltpu.make_async_remote_copy(
        src_ref=whole2, dst_ref=whole2, send_sem=send2, recv_sem=recv2,
        device_id=(lax.rem(me + 1, devices),), device_id_type=MESH,
    )
    wait2.wait_recv()
    side(s_ref, got, 1, so_ref, sl_ref, factor)
    side(t_ref, got, 0, to_ref, tl_ref, factor)
    wait1.wait_send()
    wait2.wait_send()


def local(devices, source, target, partner):
    rows, width = source.shape
    vmem = pl.BlockSpec(memory_space=pltpu.VMEM)
    so, to, sl, tl = pl.pallas_call(
        functools.partial(kernel, devices, width ** (-0.5)),
        out_shape=(
            jax.ShapeDtypeStruct((rows, width), BF),
            jax.ShapeDtypeStruct((rows, width), BF),
            jax.ShapeDtypeStruct((1, rows), F32),
            jax.ShapeDtypeStruct((1, rows), F32),
        ),
        in_specs=[pl.BlockSpec(memory_space=pltpu.SMEM), vmem, vmem],
        out_specs=(vmem, vmem, vmem, vmem),
        scratch_shapes=[
            pltpu.VMEM((devices, 16, 128), BF),
            pltpu.VMEM((devices, 2, 16, 128), BF),
            pltpu.VMEM((2, 2, rows, width), BF),
            pltpu.SemaphoreType.DMA,
            pltpu.SemaphoreType.DMA,
            pltpu.SemaphoreType.DMA,
            pltpu.SemaphoreType.DMA,
            pltpu.SemaphoreType.DMA,
        ],
        compiler_params=pltpu.CompilerParams(collective_id=0, has_side_effects=True),
    )(partner, source, target)
    return so, to, sl.reshape(rows), tl.reshape(rows)


def solution(mesh):
    devices = mesh.shape["dev"]
    return jax.shard_map(
        functools.partial(local, devices),
        mesh=mesh,
        in_specs=(P("dev", None), P("dev", None), P()),
        out_specs=(P("dev", None), P("dev", None), P("dev"), P("dev")),
        check_vma=False,
    )
```

time: 76.8 us -> 44 us (0.57)
  Pallas kernels: 0 us -> 39.6 us
  starting transfers between devices: 24.5 us -> 0 us
  waiting for transfers between devices: 23.7 us -> 0 us
  local copies, waits for them, and re-layouts: 18.6 us -> 3.6 us
  other arithmetic: 5.37 us -> 0 us
  matrix products: 3.47 us -> 0 us
    pallas_call x0 -> x1, Pallas kernels: none -> 39.6 us  [local(): pl.pallas_call(functools.partial(kernel, devices, width ** (-0.5)), out_s...]
    all_to_all x3 -> x0, starting transfers between devices: 24.5 us -> none  [the longest x1 11.5 us: sent_together(): lax.all_to_all(both, axis, split_axis=split_dim, concat_axis=concat_dim,...]
    all_to_all x3 -> x0, waiting for transfers between devices: 23.7 us -> none  [the longest x1 11.4 us: local(): lax.all_to_all(outgoing_targets, 'dev', split_axis=1, concat_axis=1, tile...]
    scatter x1 -> x0, local copies, waits for them, and re-layouts: 11.4 us -> none  [invert_row(): return jnp.zeros((blocks,), jnp.int32).at[order].set(numbers)]
    dot_general x8 -> x0, matrix products: 3.47 us -> none  [the longest x4 2.47 us: attend(): jnp.dot(weights.astype(jnp.bfloat16), values, preferred_element_type=jnp....]
    select_n x2 -> x0, other arithmetic: 3.01 us -> none  [the longest x1 1.51 us: local(): outgoing_sources = jnp.take(held_sources, inverse, axis=0)]
    unnamed x6 -> x10, local copies, waits for them, and re-layouts: 0.88 us -> 3.6 us
    gather x2 -> x0, local copies, waits for them, and re-layouts: 2.34 us -> none  [the longest x1 1.17 us: local(): outgoing_sources = jnp.take(held_sources, inverse, axis=0)]
  transfers between devices with their start and end apart: 3 -> 0, of which waited for: 3 -> 0; matrix products, arithmetic and copies ran while one was open for 22% -> 0% of each run, Pallas kernels for 0% -> 0%
where the time goes in v1:
time: 44 us; the launch traced here: 43.9 us
  Pallas kernels  39.6 us (90%)
  local copies, waits for them, and re-layouts  3.6 us (8%)
  between operations  0.65 us (1%)
    pallas_call x1, Pallas kernels, local(): pl.pallas_call(functools.partial(kernel, devices, width ** (-0.5)), out_s...  39.6 us
    unnamed x10, local copies, waits for them, and re-layouts  3.6 us

profile of v1, /device:TPU:1, one launch (start us, length us, event | category | flops | bytes accessed | tf_op | source)
XLA Modules:
  0.0 43.9 jit_solution(10693715980870920266)
XLA Ops:
  0.6 39.6 %shard_map.66 = (bf16[128,1024]{1,0:T(8,128)(2,1)}, bf16[128,1024]{1,0:T(8,128)(2,1)}, f32[1,128]{1,0:T(1,128)}, f32[1,128]{1,0:T(1,128)}) custom-call(s32[2,128]{1,0:T(2,128)} %partner.1, bf16[128,1024]{1,0:T(8,128)(2,1)} %s_ref.1, bf16[128,1024]{1,0:T(8,128)(2,1)} %t_ref.1), custom_call_target="tpu_custom_call" | custom-call | tf_op jit(solution)/shard_map/pallas_call | solution.py:135
  40.3 0.0 copy-start
  40.3 1.7 %copy.11 = bf16[128,1024]{1,0:T(8,128)(2,1)} copy(bf16[128,1024]{1,0:T(8,128)(2,1)} %get-tuple-element.16) | data formatting | bytes 524288
  42.0 0.0 copy-done
  42.0 0.0 copy-start.2
  42.0 0.7 %copy.12 = bf16[128,1024]{1,0:T(8,128)(2,1)} copy(bf16[128,1024]{1,0:T(8,128)(2,1)S(1)} %copy-done) | data formatting | bytes 524288
  42.7 0.0 copy-done.2
  42.7 0.0 copy-start.1
  42.7 0.5 %copy.13 = f32[128]{0:T(128)} copy(f32[128]{0:T(128)S(1)} %bitcast.3) | data formatting | bytes 1024
  43.2 0.1 copy-done.1
  43.4 0.5 %copy.14 = f32[128]{0:T(128)} copy(f32[128]{0:T(128)S(1)} %bitcast.2) | data formatting | bytes 1024
Async XLA Ops:
  40.3 1.7 %copy-start = (bf16[128,1024]{1,0:T(8,128)(2,1)S(1)}, bf16[128,1024]{1,0:T(8,128)(2,1)}, u32[]{:S(2)}) copy-start(bf16[128,1024]{1,0:T(8,128)(2,1)} %get-tuple-element.17) | copy-start | bytes 786436
  42.0 0.7 %copy-start.2 = (f32[1,128]{1,0:T(1,128)S(1)}, f32[1,128]{1,0:T(1,128)}, u32[]{:S(2)}) copy-start(f32[1,128]{1,0:T(1,128)} %get-tuple-element.10) | copy-start | bytes 1540
  42.7 0.7 %copy-start.1 = (f32[1,128]{1,0:T(1,128)S(1)}, f32[1,128]{1,0:T(1,128)}, u32[]{:S(2)}) copy-start(f32[1,128]{1,0:T(1,128)} %get-tuple-element.11) | copy-start | bytes 1540

commit v2 on v1

v2 whole, which is shorter than its diff:
```python
import functools

import jax
import jax.numpy as jnp
from jax import lax
from jax.experimental import pallas as pl
from jax.experimental.pallas import tpu as pltpu
from jax.sharding import PartitionSpec as P

MESH = pl.DeviceIdType.MESH
BF, F32 = jnp.bfloat16, jnp.float32
SIDE = 4
CHIPS = SIDE * SIDE * SIDE
DEVICES = 2 * CHIPS
WIDE = 256


def tile(chip):
    row = pl.multiple_of(lax.div(chip, 8) * 16, 16)
    column = pl.multiple_of(lax.rem(chip, 8) * 128, 128)
    return pl.ds(row, 16), pl.ds(column, 128)


def shifted(chip, offset):
    z = lax.rem(lax.div(chip, 16) + lax.div(offset, 16), 4)
    y = lax.rem(lax.div(chip, 4) + lax.div(offset, 4), 4)
    x = lax.rem(chip + offset, 4)
    return 16 * z + 4 * y + x


def weigh(queries, values, factor):
    scores = lax.dot_general(
        queries, values, (((1,), (1,)), ((), ())), preferred_element_type=F32
    ) * factor
    highest = jnp.max(scores, axis=1, keepdims=True)
    weights = jnp.exp(scores - highest)
    total = jnp.sum(weights, axis=1, keepdims=True)
    return highest, total, weights.astype(BF)


def to_row(column):
    rows = column.shape[0]
    at_row = lax.broadcasted_iota(jnp.int32, (rows, rows), 0)
    at_column = lax.broadcasted_iota(jnp.int32, (rows, rows), 1)
    spread = jnp.where(at_row == at_column, jnp.broadcast_to(column, (rows, rows)), 0.0)
    return jnp.sum(spread, axis=0, keepdims=True)


def kernel(
    factor, partner, s_hbm, t_hbm, so_hbm, to_hbm, lse_ref,
    s_ref, t_ref, so_ref, to_ref, first, held, stage, got,
    send1, recv1, send2, recv2, in_sem, out_sem,
):
    me = lax.axis_index("dev")
    chip, core = lax.div(me, 2), lax.rem(me, 2)
    rows, columns = tile(chip)

    get_s = pltpu.make_async_copy(s_hbm, s_ref, in_sem.at[0])
    get_t = pltpu.make_async_copy(t_hbm, t_ref, in_sem.at[1])
    get_s.start()
    get_t.start()

    barrier = pltpu.get_barrier_semaphore()

    @pl.loop(1, DEVICES)
    def _(k):
        pl.semaphore_signal(
            barrier, inc=1, device_id=(lax.rem(me + k, DEVICES),), device_id_type=MESH
        )

    get_s.wait()
    get_t.wait()
    pl.semaphore_wait(barrier, DEVICES - 1)

    def spread(ref, to_chip, to_core):
        at_rows, at_columns = tile(to_chip)
        pltpu.make_async_remote_copy(
            src_ref=ref.at[at_rows, at_columns],
            dst_ref=held.at[me],
            send_sem=send1,
            recv_sem=recv1,
            device_id=(2 * to_chip + to_core,),
            device_id_type=MESH,
        ).start()

    def keep(ref):
        pltpu.make_async_copy(ref.at[rows, columns], held.at[me], recv1).start()

    for to_core, ref in ((0, s_ref), (1, t_ref)):
        @pl.when(core == to_core)
        def _():
            keep(ref)

        @pl.when(core != to_core)
        def _():
            spread(ref, chip, to_core)

        @pl.loop(1, CHIPS)
        def _(k):
            spread(ref, shifted(chip, lax.rem(k * 27, CHIPS)), to_core)

    pltpu.make_async_copy(held, held, recv1).wait()

    def fetch(turn, j):
        stage[j, turn] = held[partner[turn, j]]

    def both(j):
        return stage.at[j], got.at[0, :, rows, columns], recv2.at[0]

    def one(turn, j):
        return stage.at[j, turn], got.at[1, turn, rows, columns], recv2.at[1 + turn]

    def collect(turns, parts):
        for turn in turns:
            fetch(turn, me)
        src, dst, sem = parts(me)
        pltpu.make_async_copy(src, dst, sem).start()

        @pl.loop(1, DEVICES)
        def _(k):
            offset = lax.rem(k * 53, DEVICES)
            j = 2 * shifted(chip, lax.div(offset, 2)) + lax.rem(core + offset, 2)
            for turn in turns:
                fetch(turn, j)
            src, dst, sem = parts(j)
            pltpu.make_async_remote_copy(
                src_ref=src, dst_ref=dst, send_sem=send2, recv_sem=sem,
                device_id=(j,), device_id_type=MESH,
            ).start()

    @pl.when(core == 0)
    def _():
        collect((0, 1), both)

    @pl.when(core == 1)
    def _():
        collect((0,), functools.partial(one, 0))
        collect((1,), functools.partial(one, 1))

    def part(which, turn, weights, at):
        return jnp.dot(weights, got[which, turn, :, at], preferred_element_type=F32)

    def merged(m0, t0, m1, t1):
        peak = jnp.maximum(m0, m1)
        f0, f1 = jnp.exp(m0 - peak), jnp.exp(m1 - peak)
        den = f0 * t0 + f1 * t1
        return f0, f1, 1.0 / den, to_row(peak + jnp.log(den))

    chunks = [slice(at, at + WIDE) for at in range(0, s_ref.shape[1], WIDE)]

    pltpu.make_async_copy(got.at[0], got.at[0], recv2.at[0]).wait()
    queries = t_ref[...]
    m0, t0, p0 = weigh(queries, got[0, 0], factor)
    m1, t1, p1 = weigh(queries, got[0, 1], factor)
    f0, f1, inverse, lse = merged(m0, t0, m1, t1)
    for at in chunks:
        to_ref[:, at] = ((f0 * part(0, 0, p0, at) + f1 * part(0, 1, p1, at)) * inverse).astype(BF)
    put_t = pltpu.make_async_copy(to_ref, to_hbm, out_sem.at[1])
    put_t.start()
    lse_ref[1:2] = lse

    pltpu.make_async_copy(got.at[1, 0], got.at[1, 0], recv2.at[1]).wait()
    queries = s_ref[...]
    m0, t0, p0 = weigh(queries, got[1, 0], factor)
    for at in chunks:
        first[:, at] = part(1, 0, p0, at)

    pltpu.make_async_copy(got.at[1, 1], got.at[1, 1], recv2.at[2]).wait()
    m1, t1, p1 = weigh(queries, got[1, 1], factor)
    f0, f1, inverse, lse = merged(m0, t0, m1, t1)
    for at in chunks:
        so_ref[:, at] = ((f0 * first[:, at] + f1 * part(1, 1, p1, at)) * inverse).astype(BF)
    put_s = pltpu.make_async_copy(so_ref, so_hbm, out_sem.at[0])
    put_s.start()
    lse_ref[0:1] = lse

    def sent(ref, sem):
        pltpu.make_async_remote_copy(
            src_ref=ref, dst_ref=ref, send_sem=sem, recv_sem=sem,
            device_id=(lax.rem(me + 1, DEVICES),), device_id_type=MESH,
        ).wait_send()

    sent(held.at[pl.ds(0, DEVICES - 1)], send1)
    sent(stage.at[pl.ds(0, DEVICES - 1)], send2)
    put_t.wait()
    put_s.wait()


def hand_on(s_ref, t_ref, lse_ref, so_ref, to_ref, sl_ref, tl_ref, s_buf, t_buf, sems):
    ins = [
        pltpu.make_async_copy(s_ref, s_buf, sems.at[0]),
        pltpu.make_async_copy(t_ref, t_buf, sems.at[1]),
    ]
    outs = [
        pltpu.make_async_copy(s_buf, so_ref, sems.at[2]),
        pltpu.make_async_copy(t_buf, to_ref, sems.at[3]),
    ]
    for copy in ins:
        copy.start()
    sl_ref[...] = lse_ref[0]
    tl_ref[...] = lse_ref[1]
    for there, back in zip(ins, outs):
        there.wait()
        back.start()
    for copy in outs:
        copy.wait()


def local(source, target, partner):
    rows, width = source.shape
    vmem = pl.BlockSpec(memory_space=pltpu.VMEM)
    anywhere = pl.BlockSpec(memory_space=pl.ANY)
    slab = jax.ShapeDtypeStruct((rows, width), BF)
    row = jax.ShapeDtypeStruct((rows,), F32)
    aligned_s, aligned_t, lse = pl.pallas_call(
        functools.partial(kernel, width ** (-0.5)),
        out_shape=(slab, slab, jax.ShapeDtypeStruct((2, rows), F32)),
        in_specs=[pl.BlockSpec(memory_space=pltpu.SMEM), anywhere, anywhere],
        out_specs=(anywhere, anywhere, vmem),
        scratch_shapes=[
            pltpu.VMEM((rows, width), BF),
            pltpu.VMEM((rows, width), BF),
            pltpu.VMEM((rows, width), BF),
            pltpu.VMEM((rows, width), BF),
            pltpu.VMEM((rows, width), F32),
            pltpu.VMEM((DEVICES, 16, 128), BF),
            pltpu.VMEM((DEVICES, 2, 16, 128), BF),
            pltpu.VMEM((2, 2, rows, width), BF),
            pltpu.SemaphoreType.DMA,
            pltpu.SemaphoreType.DMA,
            pltpu.SemaphoreType.DMA,
            pltpu.SemaphoreType.DMA((3,)),
            pltpu.SemaphoreType.DMA((2,)),
            pltpu.SemaphoreType.DMA((2,)),
        ],
        compiler_params=pltpu.CompilerParams(collective_id=0, has_side_effects=True),
    )(partner, source, target)
    return pl.pallas_call(
        hand_on,
        out_shape=(slab, slab, row, row),
        in_specs=[anywhere, anywhere, vmem],
        out_specs=(anywhere, anywhere, vmem, vmem),
        scratch_shapes=[
            pltpu.VMEM((rows, width), BF),
            pltpu.VMEM((rows, width), BF),
            pltpu.SemaphoreType.DMA((4,)),
        ],
    )(aligned_s, aligned_t, lse)


def solution(mesh):
    return jax.shard_map(
        local,
        mesh=mesh,
        in_specs=(P("dev", None), P("dev", None), P()),
        out_specs=(P("dev", None), P("dev", None), P("dev"), P("dev")),
        check_vma=False,
    )
```

time: 44 us -> 41.5 us (0.943)
  local copies, waits for them, and re-layouts: 3.6 us -> 0 us
  Pallas kernels: 39.6 us -> 40.7 us
    unnamed x10 -> x0, local copies, waits for them, and re-layouts: 3.6 us -> none
    pallas_call x1 -> x2, Pallas kernels: 39.6 us -> 40.7 us  [the longest x1 37.8 us: local(): pl.pallas_call(functools.partial(kernel, width ** (-0.5)), out_shape=(sla...]
where the time goes in v2:
time: 41.5 us; the launch traced here: 41.4 us
  Pallas kernels  40.7 us (98%)
  between operations  0.64 us (2%)
    pallas_call x1, Pallas kernels, local(): pl.pallas_call(functools.partial(kernel, width ** (-0.5)), out_shape=(sla...  37.8 us
    pallas_call x1, Pallas kernels, local(): pl.pallas_call(hand_on, out_shape=(slab, slab, row, row), in_specs=[anywh...  2.92 us

profile of v2, /device:TPU:1, one launch (start us, length us, event | category | flops | bytes accessed | tf_op | source)
XLA Modules:
  0.0 41.4 jit_solution(16788402332464028537)
XLA Ops:
  0.6 37.8 %shard_map.66 = (bf16[128,1024]{1,0:T(8,128)(2,1)}, bf16[128,1024]{1,0:T(8,128)(2,1)}, f32[2,128]{1,0:T(2,128)}) custom-call(s32[2,128]{1,0:T(2,128)} %partner.1, bf16[128,1024]{1,0:T(8,128)(2,1)} %s_hbm.1, bf16[128,1024]{1,0:T(8,128)(2,1)} %t_hbm.1), custom_call_target="tpu_custom_call" | custom-call | tf_op jit(solution)/shard_map/pallas_call | solution.py:215
  38.5 2.9 %shard_map.67 = (bf16[128,1024]{1,0:T(8,128)(2,1)}, bf16[128,1024]{1,0:T(8,128)(2,1)}, f32[128]{0:T(128)}, f32[128]{0:T(128)}) custom-call(bf16[128,1024]{1,0:T(8,128)(2,1)} %get-tuple-element.7.s_ref, bf16[128,1024]{1,0:T(8,128)(2,1)} %get-tuple-element.8.t_ref, f32[2,128]{1,0:T(2,128)} %get-tuple-element.9.lse_ref), custom_call_target="tpu_custom_call" | custom-call | tf_op jit(solution)/shard_map/pallas_call | solution.py:238

commit v3 on v2

v3 whole, which is shorter than its diff:
```python
import functools

import jax
import jax.numpy as jnp
from jax import lax
from jax.experimental import pallas as pl
from jax.experimental.pallas import tpu as pltpu
from jax.sharding import PartitionSpec as P

MESH = pl.DeviceIdType.MESH
BF, F32 = jnp.bfloat16, jnp.float32
SIDE = 4
DEVICES = 2 * SIDE**3
WIDE = 256
HOPS = (0, 1, 2, 1)
FAR_FIRST = sorted(
    ((z, y, x) for z in range(SIDE) for y in range(SIDE) for x in range(SIDE)),
    key=lambda offset: -sum(HOPS[step] for step in offset),
)[:-1]


def tile(chip):
    row = pl.multiple_of(lax.div(chip, 8) * 16, 16)
    column = pl.multiple_of(lax.rem(chip, 8) * 128, 128)
    return pl.ds(row, 16), pl.ds(column, 128)


def away(place, offset):
    z, y, x = (lax.rem(at + step, SIDE) if step else at for at, step in zip(place, offset))
    return (SIDE * z + y) * SIDE + x


def weigh(queries, values, factor):
    scores = lax.dot_general(
        queries, values, (((1,), (1,)), ((), ())), preferred_element_type=F32
    ) * factor
    highest = jnp.max(scores, axis=1, keepdims=True)
    weights = jnp.exp(scores - highest)
    total = jnp.sum(weights, axis=1, keepdims=True)
    return highest, total, weights.astype(BF)


def to_row(column):
    rows = column.shape[0]
    at_row = lax.broadcasted_iota(jnp.int32, (rows, rows), 0)
    at_column = lax.broadcasted_iota(jnp.int32, (rows, rows), 1)
    spread = jnp.where(at_row == at_column, jnp.broadcast_to(column, (rows, rows)), 0.0)
    return jnp.sum(spread, axis=0, keepdims=True)


def kernel(
    factor, partner, s_hbm, t_hbm, so_hbm, to_hbm, lse_ref,
    s_ref, t_ref, so_ref, to_ref, held, stage, got,
    send1, recv1, send2, recv2, in_sem, out_sem,
):
    me = lax.axis_index("dev")
    chip, core = lax.div(me, 2), lax.rem(me, 2)
    place = tuple(lax.rem(lax.div(chip, unit), SIDE) for unit in (SIDE * SIDE, SIDE, 1))
    mate = 2 * chip + 1 - core
    rows, columns = tile(chip)

    get_s = pltpu.make_async_copy(s_hbm, s_ref, in_sem.at[0])
    get_t = pltpu.make_async_copy(t_hbm, t_ref, in_sem.at[1])
    get_s.start()
    get_t.start()

    barrier = pltpu.get_barrier_semaphore()

    def others():
        for offset in FAR_FIRST:
            first_core = 2 * away(place, offset)
            yield first_core
            yield first_core + 1
        yield mate

    for j in others():
        pl.semaphore_signal(barrier, inc=1, device_id=(j,), device_id_type=MESH)

    get_s.wait()
    get_t.wait()
    pl.semaphore_wait(barrier, DEVICES - 1)

    def spread(ref, to_chip, to_core):
        at_rows, at_columns = tile(to_chip)
        pltpu.make_async_remote_copy(
            src_ref=ref.at[at_rows, at_columns],
            dst_ref=held.at[me],
            send_sem=send1,
            recv_sem=recv1,
            device_id=(2 * to_chip + to_core,),
            device_id_type=MESH,
        ).start()

    def keep(ref):
        pltpu.make_async_copy(ref.at[rows, columns], held.at[me], recv1).start()

    for to_core, ref in ((0, s_ref), (1, t_ref)):
        @pl.when(core == to_core)
        def _():
            keep(ref)

        @pl.when(core != to_core)
        def _():
            spread(ref, chip, to_core)

        for offset in FAR_FIRST:
            spread(ref, away(place, offset), to_core)

    pltpu.make_async_copy(held, held, recv1).wait()

    def fetch(j):
        for turn in range(2):
            stage[j, turn] = held[partner[turn, j]]

    fetch(me)
    pltpu.make_async_copy(
        stage.at[me], got.at[core, :, rows, columns], recv2.at[core]
    ).start()
    for j in others():
        fetch(j)
        pltpu.make_async_remote_copy(
            src_ref=stage.at[j],
            dst_ref=got.at[core, :, rows, columns],
            send_sem=send2,
            recv_sem=recv2.at[core],
            device_id=(j,),
            device_id_type=MESH,
        ).start()

    def part(which, turn, weights, at):
        return jnp.dot(weights, got[which, turn, :, at], preferred_element_type=F32)

    def merged(m0, t0, m1, t1):
        peak = jnp.maximum(m0, m1)
        f0, f1 = jnp.exp(m0 - peak), jnp.exp(m1 - peak)
        den = f0 * t0 + f1 * t1
        return f0, f1, 1.0 / den, to_row(peak + jnp.log(den))

    chunks = [slice(at, at + WIDE) for at in range(0, s_ref.shape[1], WIDE)]

    def side(which, query_ref, aligned_ref, slab, row):
        pltpu.make_async_copy(got.at[which], got.at[which], recv2.at[which]).wait()
        queries = query_ref[...]
        m0, t0, p0 = weigh(queries, got[which, 0], factor)
        m1, t1, p1 = weigh(queries, got[which, 1], factor)
        f0, f1, inverse, lse = merged(m0, t0, m1, t1)
        for at in chunks:
            total = f0 * part(which, 0, p0, at) + f1 * part(which, 1, p1, at)
            aligned_ref[:, at] = (total * inverse).astype(BF)
        lse_ref[row : row + 1] = lse
        put = pltpu.make_async_copy(aligned_ref, slab, out_sem.at[row])
        put.start()
        return put

    put_t = side(0, t_ref, to_ref, to_hbm, 1)
    put_s = side(1, s_ref, so_ref, so_hbm, 0)

    def sent(ref, sem):
        pltpu.make_async_remote_copy(
            src_ref=ref, dst_ref=ref, send_sem=sem, recv_sem=sem,
            device_id=(lax.rem(me + 1, DEVICES),), device_id_type=MESH,
        ).wait_send()

    sent(held.at[pl.ds(0, DEVICES - 1)], send1)
    sent(stage.at[pl.ds(0, DEVICES - 1)], send2)
    put_t.wait()
    put_s.wait()


def hand_on(s_ref, t_ref, lse_ref, so_ref, to_ref, sl_ref, tl_ref):
    so_ref[...] = s_ref[...]
    to_ref[...] = t_ref[...]
    sl_ref[...] = lse_ref[0]
    tl_ref[...] = lse_ref[1]


def local(source, target, partner):
    rows, width = source.shape
    vmem = pl.BlockSpec(memory_space=pltpu.VMEM)
    anywhere = pl.BlockSpec(memory_space=pl.ANY)
    slab = jax.ShapeDtypeStruct((rows, width), BF)
    row = jax.ShapeDtypeStruct((rows,), F32)
    aligned_s, aligned_t, lse = pl.pallas_call(
        functools.partial(kernel, width ** (-0.5)),
        out_shape=(slab, slab, jax.ShapeDtypeStruct((2, rows), F32)),
        in_specs=[pl.BlockSpec(memory_space=pltpu.SMEM), anywhere, anywhere],
        out_specs=(anywhere, anywhere, vmem),
        scratch_shapes=[
            pltpu.VMEM((rows, width), BF),
            pltpu.VMEM((rows, width), BF),
            pltpu.VMEM((rows, width), BF),
            pltpu.VMEM((rows, width), BF),
            pltpu.VMEM((DEVICES, 16, 128), BF),
            pltpu.VMEM((DEVICES, 2, 16, 128), BF),
            pltpu.VMEM((2, 2, rows, width), BF),
            pltpu.SemaphoreType.DMA,
            pltpu.SemaphoreType.DMA,
            pltpu.SemaphoreType.DMA,
            pltpu.SemaphoreType.DMA((2,)),
            pltpu.SemaphoreType.DMA((2,)),
            pltpu.SemaphoreType.DMA((2,)),
        ],
        compiler_params=pltpu.CompilerParams(collective_id=0, has_side_effects=True),
    )(partner, source, target)
    return pl.pallas_call(
        hand_on,
        out_shape=(slab, slab, row, row),
        in_specs=[vmem, vmem, vmem],
        out_specs=(vmem, vmem, vmem, vmem),
    )(aligned_s, aligned_t, lse)


def solution(mesh):
    return jax.shard_map(
        local,
        mesh=mesh,
        in_specs=(P("dev", None), P("dev", None), P()),
        out_specs=(P("dev", None), P("dev", None), P("dev"), P("dev")),
        check_vma=False,
    )
```

time: 41.5 us -> 38.3 us (0.923)
  Pallas kernels: 40.7 us -> 37.5 us
    pallas_call x1, Pallas kernels: 37.8 us -> 35.6 us  [local(): pl.pallas_call(functools.partial(kernel, width ** (-0.5)), out_shape=(sla...]
    pallas_call x1, Pallas kernels: 2.92 us -> 1.84 us  [local(): pl.pallas_call(hand_on, out_shape=(slab, slab, row, row), in_specs=[vmem,...]
where the time goes in v3:
time: 38.3 us; the launch traced here: 38.1 us
  Pallas kernels  37.5 us (98%)
  between operations  0.64 us (2%)
    pallas_call x1, Pallas kernels, local(): pl.pallas_call(functools.partial(kernel, width ** (-0.5)), out_shape=(sla...  35.6 us
    pallas_call x1, Pallas kernels, local(): pl.pallas_call(hand_on, out_shape=(slab, slab, row, row), in_specs=[vmem,...  1.84 us

profile of v3, /device:TPU:1, one launch (start us, length us, event | category | flops | bytes accessed | tf_op | source)
XLA Modules:
  0.0 38.1 jit_solution(14355041211784100641)
XLA Ops:
  0.6 35.6 %shard_map.66 = (bf16[128,1024]{1,0:T(8,128)(2,1)}, bf16[128,1024]{1,0:T(8,128)(2,1)}, f32[2,128]{1,0:T(2,128)}) custom-call(s32[2,128]{1,0:T(2,128)} %partner.1, bf16[128,1024]{1,0:T(8,128)(2,1)} %s_hbm.1, bf16[128,1024]{1,0:T(8,128)(2,1)} %t_hbm.1), custom_call_target="tpu_custom_call" | custom-call | tf_op jit(solution)/shard_map/pallas_call | solution.py:183
  36.3 1.8 %shard_map.67 = (bf16[128,1024]{1,0:T(8,128)(2,1)}, bf16[128,1024]{1,0:T(8,128)(2,1)}, f32[128]{0:T(128)}, f32[128]{0:T(128)}) custom-call(bf16[128,1024]{1,0:T(8,128)(2,1)} %get-tuple-element.7.s_ref, bf16[128,1024]{1,0:T(8,128)(2,1)} %get-tuple-element.8.t_ref, f32[2,128]{1,0:T(2,128)} %get-tuple-element.9.lse_ref), custom_call_target="tpu_custom_call" | custom-call | tf_op jit(solution)/shard_map/pallas_call | solution.py:205

commit v4 on v3

--- a/solution.py
+++ b/solution.py
@@ -12,6 +12,7 @@
 SIDE = 4
 DEVICES = 2 * SIDE**3
 WIDE = 256
+GRANT = 54700 << 10
 HOPS = (0, 1, 2, 1)
 FAR_FIRST = sorted(
     ((z, y, x) for z in range(SIDE) for y in range(SIDE) for x in range(SIDE)),
@@ -49,9 +50,9 @@
 
 
 def kernel(
-    factor, partner, s_hbm, t_hbm, so_hbm, to_hbm, lse_ref,
-    s_ref, t_ref, so_ref, to_ref, held, stage, got,
-    send1, recv1, send2, recv2, in_sem, out_sem,
+    factor, partner_hbm, s_hbm, t_hbm, so_ref, to_ref, lse_ref,
+    partner, s_ref, t_ref, held, stage, got,
+    send1, recv1, send2, recv2, in_sem,
 ):
     me = lax.axis_index("dev")
     chip, core = lax.div(me, 2), lax.rem(me, 2)
@@ -61,8 +62,10 @@
 
     get_s = pltpu.make_async_copy(s_hbm, s_ref, in_sem.at[0])
     get_t = pltpu.make_async_copy(t_hbm, t_ref, in_sem.at[1])
+    get_partner = pltpu.make_async_copy(partner_hbm, partner, in_sem.at[2])
     get_s.start()
     get_t.start()
+    get_partner.start()
 
     barrier = pltpu.get_barrier_semaphore()
 
@@ -76,6 +79,7 @@
     for j in others():
         pl.semaphore_signal(barrier, inc=1, device_id=(j,), device_id_type=MESH)
 
+    get_partner.wait()
     get_s.wait()
     get_t.wait()
     pl.semaphore_wait(barrier, DEVICES - 1)
@@ -138,7 +142,7 @@
 
     chunks = [slice(at, at + WIDE) for at in range(0, s_ref.shape[1], WIDE)]
 
-    def side(which, query_ref, aligned_ref, slab, row):
+    def side(which, query_ref, aligned_ref, row):
         pltpu.make_async_copy(got.at[which], got.at[which], recv2.at[which]).wait()
         queries = query_ref[...]
         m0, t0, p0 = weigh(queries, got[which, 0], factor)
@@ -148,12 +152,9 @@
             total = f0 * part(which, 0, p0, at) + f1 * part(which, 1, p1, at)
             aligned_ref[:, at] = (total * inverse).astype(BF)
         lse_ref[row : row + 1] = lse
-        put = pltpu.make_async_copy(aligned_ref, slab, out_sem.at[row])
-        put.start()
-        return put
-
-    put_t = side(0, t_ref, to_ref, to_hbm, 1)
-    put_s = side(1, s_ref, so_ref, so_hbm, 0)
+
+    side(0, t_ref, to_ref, 1)
+    side(1, s_ref, so_ref, 0)
 
     def sent(ref, sem):
         pltpu.make_async_remote_copy(
@@ -163,8 +164,6 @@
 
     sent(held.at[pl.ds(0, DEVICES - 1)], send1)
     sent(stage.at[pl.ds(0, DEVICES - 1)], send2)
-    put_t.wait()
-    put_s.wait()
 
 
 def hand_on(s_ref, t_ref, lse_ref, so_ref, to_ref, sl_ref, tl_ref):
@@ -183,11 +182,10 @@
     aligned_s, aligned_t, lse = pl.pallas_call(
         functools.partial(kernel, width ** (-0.5)),
         out_shape=(slab, slab, jax.ShapeDtypeStruct((2, rows), F32)),
-        in_specs=[pl.BlockSpec(memory_space=pltpu.SMEM), anywhere, anywhere],
-        out_specs=(anywhere, anywhere, vmem),
+        in_specs=[anywhere, anywhere, anywhere],
+        out_specs=(vmem, vmem, vmem),
         scratch_shapes=[
-            pltpu.VMEM((rows, width), BF),
-            pltpu.VMEM((rows, width), BF),
+            pltpu.SMEM(partner.shape, jnp.int32),
             pltpu.VMEM((rows, width), BF),
             pltpu.VMEM((rows, width), BF),
             pltpu.VMEM((DEVICES, 16, 128), BF),
@@ -197,16 +195,18 @@
             pltpu.SemaphoreType.DMA,
             pltpu.SemaphoreType.DMA,
             pltpu.SemaphoreType.DMA((2,)),
-            pltpu.SemaphoreType.DMA((2,)),
-            pltpu.SemaphoreType.DMA((2,)),
+            pltpu.SemaphoreType.DMA((3,)),
         ],
-        compiler_params=pltpu.CompilerParams(collective_id=0, has_side_effects=True),
+        compiler_params=pltpu.CompilerParams(
+            collective_id=0, has_side_effects=True, vmem_limit_bytes=GRANT
+        ),
     )(partner, source, target)
     return pl.pallas_call(
         hand_on,
         out_shape=(slab, slab, row, row),
         in_specs=[vmem, vmem, vmem],
         out_specs=(vmem, vmem, vmem, vmem),
+        compiler_params=pltpu.CompilerParams(vmem_limit_bytes=GRANT),
     )(aligned_s, aligned_t, lse)
 
 

time: 38.3 us -> 35.9 us (0.937)
  Pallas kernels: 37.5 us -> 34.5 us
  local copies, waits for them, and re-layouts: 0 us -> 0.67 us
    pallas_call x1, Pallas kernels: 35.6 us -> 33.6 us  [local(): pl.pallas_call(functools.partial(kernel, width ** (-0.5)), out_shape=(sla...]
    pallas_call x1, Pallas kernels: 1.84 us -> 0.83 us  [local(): pl.pallas_call(hand_on, out_shape=(slab, slab, row, row), in_specs=[vmem,...]
    unnamed x0 -> x2, local copies, waits for them, and re-layouts: none -> 0.67 us
where the time goes in v4:
time: 35.9 us; the launch traced here: 35.8 us
  Pallas kernels  34.5 us (96%)
  local copies, waits for them, and re-layouts  0.67 us (2%)
  between operations  0.65 us (2%)
    pallas_call x1, Pallas kernels, local(): pl.pallas_call(functools.partial(kernel, width ** (-0.5)), out_shape=(sla...  33.6 us
    pallas_call x1, Pallas kernels, local(): pl.pallas_call(hand_on, out_shape=(slab, slab, row, row), in_specs=[vmem,...  0.83 us

profile of v4, /device:TPU:1, one launch (start us, length us, event | category | flops | bytes accessed | tf_op | source)
XLA Modules:
  0.0 35.8 jit_solution(2739577334248559108)
XLA Ops:
  0.6 0.0 copy-start
  0.6 0.7 %copy-done = s32[2,128]{1,0:T(2,128)S(1)} copy-done((s32[2,128]{1,0:T(2,128)S(1)}, s32[2,128]{1,0:T(2,128)}, u32[]{:S(2)}) %copy-start) | copy-done | bytes 1048
  1.3 33.6 %shard_map.66 = (bf16[128,1024]{1,0:T(8,128)(2,1)S(1)}, bf16[128,1024]{1,0:T(8,128)(2,1)S(1)}, f32[2,128]{1,0:T(2,128)S(1)}) custom-call(s32[2,128]{1,0:T(2,128)S(1)} %copy-done, bf16[128,1024]{1,0:T(8,128)(2,1)} %s_hbm.1, bf16[128,1024]{1,0:T(8,128)(2,1)} %t_hbm.1), custom_call_target="tpu_custom_call" | custom-call | tf_op jit(solution)/shard_map/pallas_call | solution.py:182
  35.0 0.8 %shard_map.67 = (bf16[128,1024]{1,0:T(8,128)(2,1)}, bf16[128,1024]{1,0:T(8,128)(2,1)}, f32[128]{0:T(128)}, f32[128]{0:T(128)}) custom-call(bf16[128,1024]{1,0:T(8,128)(2,1)S(1)} %get-tuple-element.7.s_ref, bf16[128,1024]{1,0:T(8,128)(2,1)S(1)} %get-tuple-element.8.t_ref, f32[2,128]{1,0:T(2,128)S(1)} %get-tuple-element.9.lse_ref), custom_call_target="tpu_custom_call" | custom-call | tf_op jit(solution)/shard_map/pallas_call | solution.py:204
Async XLA Ops:
  0.6 0.7 %copy-start = (s32[2,128]{1,0:T(2,128)S(1)}, s32[2,128]{1,0:T(2,128)}, u32[]{:S(2)}) copy-start(s32[2,128]{1,0:T(2,128)} %partner_hbm.1) | copy-start | bytes 3076

commit v5 on v4

--- a/solution.py
+++ b/solution.py
@@ -20,10 +20,10 @@
 )[:-1]
 
 
-def tile(chip):
-    row = pl.multiple_of(lax.div(chip, 8) * 16, 16)
-    column = pl.multiple_of(lax.rem(chip, 8) * 128, 128)
-    return pl.ds(row, 16), pl.ds(column, 128)
+def tile(device):
+    row = pl.multiple_of(lax.div(device, 8) * 8, 8)
+    column = pl.multiple_of(lax.rem(device, 8) * 128, 128)
+    return pl.ds(row, 8), pl.ds(column, 128)
 
 
 def away(place, offset):
@@ -51,14 +51,14 @@
 
 def kernel(
     factor, partner_hbm, s_hbm, t_hbm, so_ref, to_ref, lse_ref,
-    partner, s_ref, t_ref, held, stage, got,
+    partner, s_ref, t_ref, held_s, held_t, stage, got,
     send1, recv1, send2, recv2, in_sem,
 ):
     me = lax.axis_index("dev")
     chip, core = lax.div(me, 2), lax.rem(me, 2)
     place = tuple(lax.rem(lax.div(chip, unit), SIDE) for unit in (SIDE * SIDE, SIDE, 1))
     mate = 2 * chip + 1 - core
-    rows, columns = tile(chip)
+    rows, columns = tile(me)
 
     get_s = pltpu.make_async_copy(s_hbm, s_ref, in_sem.at[0])
     get_t = pltpu.make_async_copy(t_hbm, t_ref, in_sem.at[1])
@@ -84,52 +84,44 @@
     get_t.wait()
     pl.semaphore_wait(barrier, DEVICES - 1)
 
-    def spread(ref, to_chip, to_core):
-        at_rows, at_columns = tile(to_chip)
-        pltpu.make_async_remote_copy(
-            src_ref=ref.at[at_rows, at_columns],
-            dst_ref=held.at[me],
-            send_sem=send1,
-            recv_sem=recv1,
-            device_id=(2 * to_chip + to_core,),
-            device_id_type=MESH,
+    sides = ((0, s_ref, held_s), (1, t_ref, held_t))
+
+    for which, ref, held in sides:
+        pltpu.make_async_copy(
+            ref.at[rows, columns], held.at[me], recv1.at[which]
         ).start()
-
-    def keep(ref):
-        pltpu.make_async_copy(ref.at[rows, columns], held.at[me], recv1).start()
-
-    for to_core, ref in ((0, s_ref), (1, t_ref)):
-        @pl.when(core == to_core)
-        def _():
-            keep(ref)
-
-        @pl.when(core != to_core)
-        def _():
-            spread(ref, chip, to_core)
-
-        for offset in FAR_FIRST:
-            spread(ref, away(place, offset), to_core)
-
-    pltpu.make_async_copy(held, held, recv1).wait()
-
-    def fetch(j):
-        for turn in range(2):
-            stage[j, turn] = held[partner[turn, j]]
-
-    fetch(me)
-    pltpu.make_async_copy(
-        stage.at[me], got.at[core, :, rows, columns], recv2.at[core]
-    ).start()
-    for j in others():
-        fetch(j)
-        pltpu.make_async_remote_copy(
-            src_ref=stage.at[j],
-            dst_ref=got.at[core, :, rows, columns],
-            send_sem=send2,
-            recv_sem=recv2.at[core],
-            device_id=(j,),
-            device_id_type=MESH,
+        for j in others():
+            at_rows, at_columns = tile(j)
+            pltpu.make_async_remote_copy(
+                src_ref=ref.at[at_rows, at_columns],
+                dst_ref=held.at[me],
+                send_sem=send1.at[which],
+                recv_sem=recv1.at[which],
+                device_id=(j,),
+                device_id_type=MESH,
+            ).start()
+
+    for which, ref, held in sides:
+        pltpu.make_async_copy(held, held, recv1.at[which]).wait()
+
+        def fetch(j):
+            for turn in range(2):
+                stage[which, j, turn] = held[partner[turn, j]]
+
+        fetch(me)
+        pltpu.make_async_copy(
+            stage.at[which, me], got.at[which, :, rows, columns], recv2.at[which]
         ).start()
+        for j in others():
+            fetch(j)
+            pltpu.make_async_remote_copy(
+                src_ref=stage.at[which, j],
+                dst_ref=got.at[which, :, rows, columns],
+                send_sem=send2.at[which],
+                recv_sem=recv2.at[which],
+                device_id=(j,),
+                device_id_type=MESH,
+            ).start()
 
     def part(which, turn, weights, at):
         return jnp.dot(weights, got[which, turn, :, at], preferred_element_type=F32)
@@ -162,8 +154,9 @@
             device_id=(lax.rem(me + 1, DEVICES),), device_id_type=MESH,
         ).wait_send()
 
-    sent(held.at[pl.ds(0, DEVICES - 1)], send1)
-    sent(stage.at[pl.ds(0, DEVICES - 1)], send2)
+    for which, ref, held in sides:
+        sent(held.at[pl.ds(0, DEVICES - 1)], send1.at[which])
+        sent(stage.at[which, pl.ds(0, DEVICES - 1)], send2.at[which])
 
 
 def hand_on(s_ref, t_ref, lse_ref, so_ref, to_ref, sl_ref, tl_ref):
@@ -188,12 +181,13 @@
             pltpu.SMEM(partner.shape, jnp.int32),
             pltpu.VMEM((rows, width), BF),
             pltpu.VMEM((rows, width), BF),
-            pltpu.VMEM((DEVICES, 16, 128), BF),
-            pltpu.VMEM((DEVICES, 2, 16, 128), BF),
+            pltpu.VMEM((DEVICES, 8, 128), BF),
+            pltpu.VMEM((DEVICES, 8, 128), BF),
+            pltpu.VMEM((2, DEVICES, 2, 8, 128), BF),
             pltpu.VMEM((2, 2, rows, width), BF),
-            pltpu.SemaphoreType.DMA,
-            pltpu.SemaphoreType.DMA,
-            pltpu.SemaphoreType.DMA,
+            pltpu.SemaphoreType.DMA((2,)),
+            pltpu.SemaphoreType.DMA((2,)),
+            pltpu.SemaphoreType.DMA((2,)),
             pltpu.SemaphoreType.DMA((2,)),
             pltpu.SemaphoreType.DMA((3,)),
         ],

time: 35.9 us -> 34.5 us (0.961)
  Pallas kernels: 34.5 us -> 33 us
    pallas_call x1, Pallas kernels: 33.6 us -> 32.2 us  [local(): pl.pallas_call(functools.partial(kernel, width ** (-0.5)), out_shape=(sla...]
where the time goes in v5:
time: 34.5 us; the launch traced here: 34.3 us
  Pallas kernels  33 us (96%)
  local copies, waits for them, and re-layouts  0.67 us (2%)
  between operations  0.65 us (2%)
    pallas_call x1, Pallas kernels, local(): pl.pallas_call(functools.partial(kernel, width ** (-0.5)), out_shape=(sla...  32.2 us
    pallas_call x1, Pallas kernels, local(): pl.pallas_call(hand_on, out_shape=(slab, slab, row, row), in_specs=[vmem,...  0.83 us

profile of v5, /device:TPU:1, one launch (start us, length us, event | category | flops | bytes accessed | tf_op | source)
XLA Modules:
  0.0 34.3 jit_solution(10667069372243574085)
XLA Ops:
  0.6 0.0 copy-start
  0.6 0.7 %copy-done = s32[2,128]{1,0:T(2,128)S(1)} copy-done((s32[2,128]{1,0:T(2,128)S(1)}, s32[2,128]{1,0:T(2,128)}, u32[]{:S(2)}) %copy-start) | copy-done | bytes 1048
  1.3 32.2 %shard_map.66 = (bf16[128,1024]{1,0:T(8,128)(2,1)S(1)}, bf16[128,1024]{1,0:T(8,128)(2,1)S(1)}, f32[2,128]{1,0:T(2,128)S(1)}) custom-call(s32[2,128]{1,0:T(2,128)S(1)} %copy-done, bf16[128,1024]{1,0:T(8,128)(2,1)} %s_hbm.1, bf16[128,1024]{1,0:T(8,128)(2,1)} %t_hbm.1), custom_call_target="tpu_custom_call" | custom-call | tf_op jit(solution)/shard_map/pallas_call | solution.py:175
  33.5 0.8 %shard_map.67 = (bf16[128,1024]{1,0:T(8,128)(2,1)}, bf16[128,1024]{1,0:T(8,128)(2,1)}, f32[128]{0:T(128)}, f32[128]{0:T(128)}) custom-call(bf16[128,1024]{1,0:T(8,128)(2,1)S(1)} %get-tuple-element.7.s_ref, bf16[128,1024]{1,0:T(8,128)(2,1)S(1)} %get-tuple-element.8.t_ref, f32[2,128]{1,0:T(2,128)S(1)} %get-tuple-element.9.lse_ref), custom_call_target="tpu_custom_call" | custom-call | tf_op jit(solution)/shard_map/pallas_call | solution.py:198
Async XLA Ops:
  0.6 0.7 %copy-start = (s32[2,128]{1,0:T(2,128)S(1)}, s32[2,128]{1,0:T(2,128)}, u32[]{:S(2)}) copy-start(s32[2,128]{1,0:T(2,128)} %partner_hbm.1) | copy-start | bytes 3076

commit v6 on v5

--- a/solution.py
+++ b/solution.py
@@ -79,7 +79,6 @@
     for j in others():
         pl.semaphore_signal(barrier, inc=1, device_id=(j,), device_id_type=MESH)
 
-    get_partner.wait()
     get_s.wait()
     get_t.wait()
     pl.semaphore_wait(barrier, DEVICES - 1)
@@ -101,6 +100,7 @@
                 device_id_type=MESH,
             ).start()
 
+    get_partner.wait()
     for which, ref, held in sides:
         pltpu.make_async_copy(held, held, recv1.at[which]).wait()
 

time: 34.5 us -> 34.5 us (level)
  no operation moved by 1% of the time
where the time goes in v6:
time: 34.5 us; the launch traced here: 34.3 us
  Pallas kernels  33 us (96%)
  local copies, waits for them, and re-layouts  0.67 us (2%)
  between operations  0.65 us (2%)
    pallas_call x1, Pallas kernels, local(): pl.pallas_call(functools.partial(kernel, width ** (-0.5)), out_shape=(sla...  32.2 us
    pallas_call x1, Pallas kernels, local(): pl.pallas_call(hand_on, out_shape=(slab, slab, row, row), in_specs=[vmem,...  0.83 us

profile of v6, /device:TPU:1, one launch (start us, length us, event | category | flops | bytes accessed | tf_op | source)
XLA Modules:
  0.0 34.3 jit_solution(11106684479190059477)
XLA Ops:
  0.6 0.0 copy-start
  0.6 0.7 %copy-done = s32[2,128]{1,0:T(2,128)S(1)} copy-done((s32[2,128]{1,0:T(2,128)S(1)}, s32[2,128]{1,0:T(2,128)}, u32[]{:S(2)}) %copy-start) | copy-done | bytes 1048
  1.3 32.2 %shard_map.66 = (bf16[128,1024]{1,0:T(8,128)(2,1)S(1)}, bf16[128,1024]{1,0:T(8,128)(2,1)S(1)}, f32[2,128]{1,0:T(2,128)S(1)}) custom-call(s32[2,128]{1,0:T(2,128)S(1)} %copy-done, bf16[128,1024]{1,0:T(8,128)(2,1)} %s_hbm.1, bf16[128,1024]{1,0:T(8,128)(2,1)} %t_hbm.1), custom_call_target="tpu_custom_call" | custom-call | tf_op jit(solution)/shard_map/pallas_call | solution.py:175
  33.5 0.8 %shard_map.67 = (bf16[128,1024]{1,0:T(8,128)(2,1)}, bf16[128,1024]{1,0:T(8,128)(2,1)}, f32[128]{0:T(128)}, f32[128]{0:T(128)}) custom-call(bf16[128,1024]{1,0:T(8,128)(2,1)S(1)} %get-tuple-element.7.s_ref, bf16[128,1024]{1,0:T(8,128)(2,1)S(1)} %get-tuple-element.8.t_ref, f32[2,128]{1,0:T(2,128)S(1)} %get-tuple-element.9.lse_ref), custom_call_target="tpu_custom_call" | custom-call | tf_op jit(solution)/shard_map/pallas_call | solution.py:198
Async XLA Ops:
  0.6 0.7 %copy-start = (s32[2,128]{1,0:T(2,128)S(1)}, s32[2,128]{1,0:T(2,128)}, u32[]{:S(2)}) copy-start(s32[2,128]{1,0:T(2,128)} %partner_hbm.1) | copy-start | bytes 3076
